TPU v7x, 32 devices: a whole 2x2x4 slice. The times are simulated.
32 devices in a mesh: cols: 8 (over z, x), rows: 4 (over y, core).
Axes of the slice: x: 2, y: 2, z: 4, core: 2. Of those that a mesh axis runs over, the one named last changes fastest.
Arguments:
- slide_pixels: bfloat16 [3, 1024, 4096], P(None, 'rows', 'cols'), may hold values from -6 to 6
- stem_first: bfloat16 [6, 6, 3, 64], replicated, may hold values from -0.625 to 0.625
- stem_second: bfloat16 [6, 6, 64, 256], replicated, may hold values from -0.125 to 0.125
- stem_third: bfloat16 [3, 3, 256, 1024], replicated, may hold values from -0.125 to 0.125
- key_weight: bfloat16 [1024, 1024], replicated, may hold values from -0.1875 to 0.1875
- value_weight: bfloat16 [1024, 1024], replicated, may hold values from -0.1875 to 0.1875
- queries: bfloat16 [512, 1024], replicated, may hold values from -240 to 240
Outputs:
- attended: bfloat16 [512, 1024], P(('cols', 'rows'))
All inputs are finite; a program needn't handle non-finite values.
Results may differ from a plain program's by a relative error of at most 0.033.
Values may be sent and summed in bfloat16 or wider, within the bound.
No kernel may reach another device: no remote copies, remote signals or barrier semaphores. Data moves between devices by JAX's collectives and lax.ppermute only.
A program may use at most 128 MiB of HBM per device.

v0:
```python
import math
import jax
import jax.numpy as jnp
from jax import lax
from jax.sharding import PartitionSpec as P

HEADS = 8


def with_halo(shard, sides, width):
    for axis, dim in sides:
        size, length = (lax.axis_size(axis), shard.shape[dim])
        up = [(i, (i + 1) % size) for i in range(size - 1)]
        down = [(j, i) for i, j in up]
        last = lax.slice_in_dim(shard, length - width, length, axis=dim)
        leading = lax.slice_in_dim(shard, 0, width, axis=dim)
        before = lax.ppermute(last, axis, up)
        after = lax.ppermute(leading, axis, down)
        shard = jnp.concatenate([before, shard, after], axis=dim)
    return shard


def shifted(value, axis, steps):
    count = lax.axis_size(axis)
    leading, last = (max(0, -steps), min(count, count - steps))
    return lax.ppermute(value, axis, [(source, source + steps) for source in range(leading, last)])


def extend(features):
    return with_halo(features, (("cols", 2), ("rows", 1)), 1)


def convolve(features, kernel, stride, layout):
    return lax.conv_general_dilated(
        features[None],
        kernel,
        (stride, stride),
        "VALID",
        dimension_numbers=layout,
        preferred_element_type=jnp.float32,
    )[0]


def norm_rows(features):
    tok_mean = jnp.mean(features, axis=-1, keepdims=True)
    centred = features - tok_mean
    tok_var = jnp.mean(centred * centred, axis=-1, keepdims=True)
    return (centred * lax.rsqrt(tok_var + 1e-05)).astype(jnp.bfloat16)


def on_device(slide_pixels, stem_first, stem_second, stem_third, key_weight, value_weight, queries):
    first_map = jax.nn.gelu(
        convolve(extend(slide_pixels), stem_first, 4, ("NCHW", "HWIO", "NCHW"))
    ).astype(jnp.bfloat16)
    second_map = jax.nn.gelu(
        convolve(extend(first_map), stem_second, 4, ("NCHW", "HWIO", "NHWC"))
    ).astype(jnp.bfloat16)
    upper_rim = shifted(second_map[-1:], "rows", 1)
    second_map = jnp.concatenate([upper_rim, second_map], axis=0)
    left_rim = shifted(second_map[:, -1:], "cols", 1)
    second_map = jnp.concatenate([left_rim, second_map], axis=1)
    third_map = convolve(second_map, stem_third, 2, ("NHWC", "HWIO", "NHWC"))
    model_width = third_map.shape[-1]
    normed = norm_rows(third_map.reshape(-1, model_width))
    tok_count = normed.shape[0]
    key_rows = jnp.dot(normed, key_weight, preferred_element_type=jnp.float32).astype(jnp.bfloat16)
    value_rows = jnp.dot(normed, value_weight, preferred_element_type=jnp.float32).astype(
        jnp.bfloat16
    )
    head_size = model_width // HEADS
    latent_count = queries.shape[0]
    query_heads = queries.reshape(latent_count, HEADS, head_size)
    scores = jnp.einsum(
        "lhd,thd->hlt",
        query_heads,
        key_rows.reshape(tok_count, HEADS, head_size),
        preferred_element_type=jnp.float32,
    ) * (1.0 / math.sqrt(head_size))
    peak_score = lax.pmax(jnp.max(scores, axis=2), ("cols", "rows"))
    weights = jnp.exp(scores - peak_score[:, :, None])
    row_total = jnp.sum(weights, axis=2).T
    rounded = weights.astype(jnp.bfloat16)
    weighted = jnp.einsum(
        "hlt,thd->lhd",
        rounded,
        value_rows.reshape(tok_count, HEADS, head_size),
        preferred_element_type=jnp.float32,
    ).reshape(latent_count, model_width)
    share_rows = latent_count // lax.axis_size(("cols", "rows"))
    weighted, row_total = lax.psum((weighted, row_total), ("cols", "rows"))
    share_start = lax.axis_index(("cols", "rows")) * share_rows
    weighted = lax.dynamic_slice_in_dim(weighted, share_start, share_rows, 0)
    row_total = lax.dynamic_slice_in_dim(row_total, share_start, share_rows, 0)
    attended = weighted.reshape(share_rows, HEADS, head_size) / row_total[:, :, None]
    return attended.reshape(share_rows, model_width).astype(jnp.bfloat16)


def solution(mesh):
    placed = (P(None, "rows", "cols"), P(), P(), P(), P(), P(), P())
    return jax.shard_map(
        on_device, mesh=mesh, in_specs=placed, out_specs=P(("cols", "rows"), None), check_vma=False
    )
```

profile of v0, /device:TPU:0, one launch (start us, length us, event | category | flops | bytes accessed | tf_op | source)
XLA Modules:
  0.0 329.5 jit_solution(13825358691176323215)
XLA Ops:
  7.8 4.9 %collective-permute-start = (bf16[3,256,1]{2,1,0:T(8,128)(2,1)S(1)}, bf16[3,256,1]{2,1,0:T(8,128)(2,1)S(1)}, u32[]{:S(2)}, u32[]{:S(2)}) collective-permute-start(bf16[3,256,1]{2,1,0:T(8,128)(2,1)S(1)} %get-tuple-element.13), channel_id=1, source_target_pairs={{0,4},{4,8},{8,12},{12,16},{16,20},{20,24},{24,28},{1,5},{5,9},{9,... | collective-permute-start | bytes 4616 | tf_op jit(solution)/shard_map/ppermute | solution.py:17
  14.0 2.9 collective-permute-done
  16.9 4.0 %collective-permute-done.1 = bf16[3,256,1]{2,1,0:T(8,128)(2,1)S(1)} collective-permute-done((bf16[3,256,1]{2,1,0:T(8,128)(2,1)S(1)}, bf16[3,256,1]{2,1,0:T(8,128)(2,1)S(1)}, u32[]{:S(2)}, u32[]{:S(2)}) %collective-permute-start.1) | collective-permute-done | bytes 1568 | tf_op jit(solution)/shard_map/ppermute | solution.py:18
  24.4 3.5 %collective-permute-done.3 = bf16[3,1,514]{2,1,0:T(2,128)(2,1)S(1)} collective-permute-done((bf16[3,1,514]{2,1,0:T(2,128)(2,1)S(1)}, bf16[3,1,514]{2,1,0:T(2,128)(2,1)S(1)}, u32[]{:S(2)}, u32[]{:S(2)}) %collective-permute-start.3) | collective-permute-done | bytes 3116 | tf_op jit(solution)/shard_map/ppermute | solution.py:18
  28.9 2.8 reshape.95
  31.7 19.5 %copy.95 = bf16[3,258,1,8,68]{3,0,4,1,2:T(4,128)(2,1)} copy(bf16[3,258,1,8,68]{4,3,1,0,2:T(8,128)(2,1)} %reshape.95) | data formatting | bytes 1684224 | tf_op jit(solution)/shard_map/conv_general_dilated | solution.py:34
  51.1 2.1 slice.46
  53.3 23.5 %broadcast_select_fusion = f32[64,8,17,64]{3,1,2,0:T(8,128)S(1)} fusion(pred[8,17]{0,1:T(8,128)(4,1)S(1)} %copy-done.5, bf16[6,6,3,64]{3,2,1,0:T(4,128)(2,1)S(1)} %copy-done.4, bf16[3,258,1,7,5]{3,0,4,1,2:T(4,128)(2,1)S(1)} %slice.46, bf16[3,258,1,8,68]{3,0,4,1,2:T(4,128)(2,1)} %copy.95), kind=kOutput, calls=%fused_computation.25 | convolution fusion | flops 123593248 | bytes 3138476 | tf_op jit(solution)/shard_map/conv_general_dilated | solution.py:34
  77.6 1.4 fusion.14
  79.0 4.5 %collective-permute-start.4 = (bf16[64,64,1]{0,1,2:T(8,128)(2,1)S(1)}, bf16[64,64,1]{0,1,2:T(8,128)(2,1)S(1)}, u32[]{:S(2)}, u32[]{:S(2)}) collective-permute-start(bf16[64,64,1]{0,1,2:T(8,128)(2,1)S(1)} %get-tuple-element.7), channel_id=1, source_target_pairs={{0,4},{4,8},{8,12},{12,16},{16,20},{20,24},{24,28},{1,5},{5,9},{9,... | collective-permute-start | bytes 24584 | tf_op jit(solution)/shard_map/ppermute | solution.py:17
  84.9 4.6 %collective-permute-done.5 = bf16[64,64,1]{0,1,2:T(8,128)(2,1)S(1)} collective-permute-done((bf16[64,64,1]{0,1,2:T(8,128)(2,1)S(1)}, bf16[64,64,1]{0,1,2:T(8,128)(2,1)S(1)}, u32[]{:S(2)}, u32[]{:S(2)}) %collective-permute-start.5) | collective-permute-done | bytes 8224 | tf_op jit(solution)/shard_map/ppermute | solution.py:18
  89.7 3.2 collective-permute-start.6
  92.9 1.5 collective-permute-start.7
  94.4 2.3 collective-permute-done.7
  96.7 4.0 %maximum_bitcast_fusion = bf16[64,66,1,130]{0,1,3,2:T(8,128)(2,1)} fusion(bf16[64,1,130]{0,1,2:T(2,128)(2,1)S(1)} %collective-permute-done.7, bf16[64,64,1]{0,1,2:T(8,128)(2,1)S(1)} %collective-permute-done.5, bf16[64,64,128]{0,1,2:T(8,128)(2,1)S(1)} %fusion.14, bf16[64,64,1]{0,1,2:T(8,128)(2,1)S(1)} %collective-permute-done.4, ...), kind=kLoop, calls=%fused_computation.24 | loop fusion | flops 5491200 | bytes 2196480 | tf_op jit(solution)/shard_map/broadcast_in_dim | solution.py:35
  100.7 4.4 %copy.122 = bf16[64,66,1,130]{1,0,3,2:T(8,128)(2,1)} copy(bf16[64,66,1,130]{0,1,3,2:T(8,128)(2,1)} %maximum_bitcast_fusion) | data formatting | bytes 2196480
  105.0 3.9 %pad.2.clone = bf16[64,66,1,160]{1,0,3,2:T(8,128)(2,1)} pad(bf16[64,66,1,130]{1,0,3,2:T(8,128)(2,1)} %copy.122, bf16[]{:T(256)} %constant.41), padding=0_0x0_0x0_0x0_30 | pad | bytes 2449922 | tf_op jit(solution)/shard_map/broadcast_in_dim | solution.py:35
  108.9 4.9 %copy.99 = bf16[64,66,1,8,20]{0,3,4,1,2:T(8,128)(2,1)} copy(bf16[64,66,1,8,20]{1,0,4,3,2:T(8,128)(2,1)} %bitcast.93) | data formatting | bytes 2703360 | tf_op jit(solution)/shard_map/conv_general_dilated | solution.py:34
  113.8 1.4 slice.50
  115.3 3.0 fusion.28
  118.7 4.8 %collective-permute-start.8 = (bf16[1,32,256]{2,0,1:T(2,128)(2,1)S(1)}, bf16[1,32,256]{2,0,1:T(2,128)(2,1)S(1)}, u32[]{:S(2)}, u32[]{:S(2)}) collective-permute-start(bf16[1,32,256]{2,0,1:T(2,128)(2,1)S(1)} %slice.52), channel_id=1, source_target_pairs={{0,1},{1,2},{2,3},{4,5},{5,6},{6,7},{8,9},{9,10},{10,11},{12,13},{... | collective-permute-start | bytes 49160 | tf_op jit(solution)/shard_map/ppermute | solution.py:26
  124.4 4.8 %collective-permute-start.9 = (bf16[17,1,256]{2,0,1:T(8,128)(2,1)S(1)}, bf16[17,1,256]{2,0,1:T(8,128)(2,1)S(1)}, u32[]{:S(2)}, u32[]{:S(2)}) collective-permute-start(bf16[17,1,256]{2,0,1:T(8,128)(2,1)S(1)} %pad_maximum_fusion.3), channel_id=1, source_target_pairs={{0,4},{4,8},{8,12},{12,16},{16,20},{20,24},{24,28},{1,5},{5,9},{9,... | collective-permute-start | bytes 26120 | tf_op jit(solution)/shard_map/ppermute | solution.py:26
  129.2 1.4 collective-permute-done.9
  134.6 1.8 bitcast_reduce_fusion
  136.4 42.2 %pmax.7 = f32[8,512]{1,0:T(8,128)S(1)} all-reduce(f32[8,512]{1,0:T(8,128)S(1)} %get-tuple-element.15), channel_id=1, replica_groups=mesh['cols'=8,'rows'=4] {'cols','rows'}, use_global_device_ids=true, to_apply=%region_3.0 | all-reduce | flops 4096 | bytes 32768 | tf_op jit(solution)/shard_map/pmax | solution.py:79
  178.6 2.0 convolution_convert_fusion.1
  180.8 3.4 %fusion.33 = f32[8,128,512]{2,1,0:T(8,128)} fusion(bf16[128,8,128]{0,2,1:T(8,128)(2,1)S(1)} %bitcast.99, f32[8,128,512]{2,1,0:T(8,128)} %get-tuple-element.16, f32[8,512]{1,0:T(8,128)S(1)} %pmax.7), kind=kOutput, calls=%fused_computation.39 | convolution fusion | flops 135790592 | bytes 4472832 | tf_op jit(solution)/shard_map/hlt,thd->lhd/dot_general | solution.py:83
  184.2 2.9 copy.113
  187.2 2.0 fusion.25
  189.1 40.1 %psum.15 = f32[512,8]{0,1:T(8,128)S(1)} all-reduce(f32[512,8]{0,1:T(8,128)S(1)} %bitcast.101), channel_id=1, replica_groups=mesh['cols'=8,'rows'=4] {'cols','rows'}, use_global_device_ids=true, to_apply=%region_6.0 | all-reduce | flops 4096 | bytes 32768 | tf_op jit(solution)/shard_map/psum | solution.py:90
  229.4 91.8 %all-reduce.2.cloned.1.call-done = f32[512,1024]{1,0:T(8,128)} async-done(((f32[512,1024]{1,0:T(8,128)}), f32[512,1024]{1,0:T(8,128)}) %all-reduce.2.cloned.1.call-update) | async-done | bytes 2097168 | tf_op jit(solution)/shard_map/psum | solution.py:90
  321.2 1.5 fusion.61
  (64 shorter events, 15.0 us)
Async XLA Ops:
  6.5 127.3 %copy-start = (bf16[1024,1024]{1,0:T(8,128)(2,1)S(1)}, bf16[1024,1024]{1,0:T(8,128)(2,1)}, u32[]{:S(2)}) copy-start(bf16[1024,1024]{1,0:T(8,128)(2,1)} %param.11) | copy-start | bytes 6291460
  6.5 21.4 %copy-start.1 = (bf16[3,256,512]{2,1,0:T(8,128)(2,1)S(1)}, bf16[3,256,512]{2,1,0:T(8,128)(2,1)}, u32[]{:S(2)}) copy-start(bf16[3,256,512]{2,1,0:T(8,128)(2,1)} %param.7) | copy-start | bytes 2359300
  6.5 314.6 %all-reduce.2.cloned.1.call-start = ((), (), s32[]{:S(2)}) async-start(), calls=%async_computation | async-start | bytes 4194304 | tf_op jit(solution)/shard_map/psum | solution.py:90
  7.8 9.1 %collective-permute-start = (bf16[3,256,1]{2,1,0:T(8,128)(2,1)S(1)}, bf16[3,256,1]{2,1,0:T(8,128)(2,1)S(1)}, u32[]{:S(2)}, u32[]{:S(2)}) collective-permute-start(bf16[3,256,1]{2,1,0:T(8,128)(2,1)S(1)} %get-tuple-element.13), channel_id=1, source_target_pairs={{0,4},{4,8},{8,12},{12,16},{16,20},{20,24},{24,28},{1,5},{5,9},{9,... | collective-permute-start | bytes 4616 | tf_op jit(solution)/shard_map/ppermute | solution.py:17
  12.7 8.3 %collective-permute-start.1 = (bf16[3,256,1]{2,1,0:T(8,128)(2,1)S(1)}, bf16[3,256,1]{2,1,0:T(8,128)(2,1)S(1)}, u32[]{:S(2)}, u32[]{:S(2)}) collective-permute-start(bf16[3,256,1]{2,1,0:T(8,128)(2,1)S(1)} %get-tuple-element.14), channel_id=1, source_target_pairs={{4,0},{8,4},{12,8},{16,12},{20,16},{24,20},{28,24},{5,1},{9,5},{13... | collective-permute-start | bytes 4616 | tf_op jit(solution)/shard_map/ppermute | solution.py:18
  21.8 2.6 collective-permute-start.2
  23.1 4.8 %collective-permute-start.3 = (bf16[3,1,514]{2,1,0:T(2,128)(2,1)S(1)}, bf16[3,1,514]{2,1,0:T(2,128)(2,1)S(1)}, u32[]{:S(2)}, u32[]{:S(2)}) collective-permute-start(bf16[3,1,514]{2,1,0:T(2,128)(2,1)S(1)} %get-tuple-element.10), channel_id=1, source_target_pairs={{1,0},{2,1},{3,2},{5,4},{6,5},{7,6},{9,8},{10,9},{11,10},{13,12},{... | collective-permute-start | bytes 9260 | tf_op jit(solution)/shard_map/ppermute | solution.py:18
  51.1 2.1 copy-start.4
  51.1 2.1 copy-start.5
  79.0 5.9 %collective-permute-start.4 = (bf16[64,64,1]{0,1,2:T(8,128)(2,1)S(1)}, bf16[64,64,1]{0,1,2:T(8,128)(2,1)S(1)}, u32[]{:S(2)}, u32[]{:S(2)}) collective-permute-start(bf16[64,64,1]{0,1,2:T(8,128)(2,1)S(1)} %get-tuple-element.7), channel_id=1, source_target_pairs={{0,4},{4,8},{8,12},{12,16},{16,20},{20,24},{24,28},{1,5},{5,9},{9,... | collective-permute-start | bytes 24584 | tf_op jit(solution)/shard_map/ppermute | solution.py:17
  83.5 6.1 %collective-permute-start.5 = (bf16[64,64,1]{0,1,2:T(8,128)(2,1)S(1)}, bf16[64,64,1]{0,1,2:T(8,128)(2,1)S(1)}, u32[]{:S(2)}, u32[]{:S(2)}) collective-permute-start(bf16[64,64,1]{0,1,2:T(8,128)(2,1)S(1)} %get-tuple-element.8), channel_id=1, source_target_pairs={{4,0},{8,4},{12,8},{16,12},{20,16},{24,20},{28,24},{5,1},{9,5},{13... | collective-permute-start | bytes 24584 | tf_op jit(solution)/shard_map/ppermute | solution.py:18
  89.7 4.6 %collective-permute-start.6 = (bf16[64,1,130]{0,1,2:T(2,128)(2,1)S(1)}, bf16[64,1,130]{0,1,2:T(2,128)(2,1)S(1)}, u32[]{:S(2)}, u32[]{:S(2)}) collective-permute-start(bf16[64,1,130]{0,1,2:T(2,128)(2,1)S(1)} %get-tuple-element.5), channel_id=1, source_target_pairs={{0,1},{1,2},{2,3},{4,5},{5,6},{6,7},{8,9},{9,10},{10,11},{12,13},{... | collective-permute-start | bytes 49928 | tf_op jit(solution)/shard_map/ppermute | solution.py:17
  92.9 3.8 %collective-permute-start.7 = (bf16[64,1,130]{0,1,2:T(2,128)(2,1)S(1)}, bf16[64,1,130]{0,1,2:T(2,128)(2,1)S(1)}, u32[]{:S(2)}, u32[]{:S(2)}) collective-permute-start(bf16[64,1,130]{0,1,2:T(2,128)(2,1)S(1)} %get-tuple-element.6), channel_id=1, source_target_pairs={{1,0},{2,1},{3,2},{5,4},{6,5},{7,6},{9,8},{10,9},{11,10},{13,12},{... | collective-permute-start | bytes 49928 | tf_op jit(solution)/shard_map/ppermute | solution.py:18
  108.9 6.3 %copy-start.3 = (bf16[6,6,64,256]{3,2,1,0:T(8,128)(2,1)S(1)}, bf16[6,6,64,256]{3,2,1,0:T(8,128)(2,1)}, u32[]{:S(2)}) copy-start(bf16[6,6,64,256]{3,2,1,0:T(8,128)(2,1)} %param.9) | copy-start | bytes 3538948
  108.9 6.3 %copy-start.6 = (pred[8,5]{0,1:T(8,128)(4,1)S(1)}, pred[8,5]{0,1:T(8,128)(4,1)}, u32[]{:S(2)}) copy-start(pred[8,5]{0,1:T(8,128)(4,1)} %constant.54) | copy-start | bytes 124
  113.8 17.2 %slice-start = ((s8[4718592]{0:T(1024)(128)(4,1)}), s8[4194304]{0:T(1024)(128)(4,1)S(1)}, s32[]{:S(2)}) async-start(s8[4718592]{0:T(1024)(128)(4,1)} %bitcast.102), calls=%async_computation.1 | async-start | bytes 8388608
  115.3 15.8 %slice-start.1 = ((s8[4718592]{0:T(1024)(128)(4,1)}), s8[524288]{0:T(1024)(128)(4,1)S(1)}, s32[]{:S(2)}) async-start(s8[4718592]{0:T(1024)(128)(4,1)} %bitcast.102), calls=%async_computation.2 | async-start | bytes 1048576
  118.5 12.6 %copy-start.7 = (pred[8,3]{0,1:T(4,128)(4,1)S(1)}, pred[8,3]{0,1:T(4,128)(4,1)}, u32[]{:S(2)}) copy-start(pred[8,3]{0,1:T(4,128)(4,1)} %constant.53) | copy-start | bytes 76
  118.7 5.7 %collective-permute-start.8 = (bf16[1,32,256]{2,0,1:T(2,128)(2,1)S(1)}, bf16[1,32,256]{2,0,1:T(2,128)(2,1)S(1)}, u32[]{:S(2)}, u32[]{:S(2)}) collective-permute-start(bf16[1,32,256]{2,0,1:T(2,128)(2,1)S(1)} %slice.52), channel_id=1, source_target_pairs={{0,1},{1,2},{2,3},{4,5},{5,6},{6,7},{8,9},{9,10},{10,11},{12,13},{... | collective-permute-start | bytes 49160 | tf_op jit(solution)/shard_map/ppermute | solution.py:26
  124.4 6.2 %collective-permute-start.9 = (bf16[17,1,256]{2,0,1:T(8,128)(2,1)S(1)}, bf16[17,1,256]{2,0,1:T(8,128)(2,1)S(1)}, u32[]{:S(2)}, u32[]{:S(2)}) collective-permute-start(bf16[17,1,256]{2,0,1:T(8,128)(2,1)S(1)} %pad_maximum_fusion.3), channel_id=1, source_target_pairs={{0,4},{4,8},{8,12},{12,16},{16,20},{20,24},{24,28},{1,5},{5,9},{9,... | collective-permute-start | bytes 26120 | tf_op jit(solution)/shard_map/ppermute | solution.py:26
  133.4 1.2 copy-start.2
Sparse Core Ops, SparseCore 0:
  187.3 133.8 all-reduce.1
where the time goes:
time: 332 us; the launch traced here: 330 us
  waiting for transfers between devices  112 us (34%)
  blocking collectives  82.2 us (25%)
  local copies, waits for them, and re-layouts  46.4 us (14%)
  matrix products  35.3 us (11%)
  starting transfers between devices  28.8 us (9%)
  between operations  13.8 us (4%)
  other arithmetic  11.4 us (3%)
    psum x1, waiting for transfers between devices, on_device(): weighted, row_total = lax.psum((weighted, row_total), ('cols', 'rows'))  91.8 us
    pmax x1, blocking collectives, on_device(): peak_score = lax.pmax(jnp.max(scores, axis=2), ('cols', 'rows'))  42.2 us
    psum x1, blocking collectives, on_device(): weighted, row_total = lax.psum((weighted, row_total), ('cols', 'rows'))  40.1 us
    conv_general_dilated x11, local copies, waits for them, and re-layouts, convolve(): lax.conv_general_dilated(features[None], kernel, (stride, stride), 'VALID...  32.7 us
    conv_general_dilated x3, matrix products, convolve(): lax.conv_general_dilated(features[None], kernel, (stride, stride), 'VALID...  27.6 us
    ppermute x4, waiting for transfers between devices, with_halo(): after = lax.ppermute(leading, axis, down)  14.5 us
    ppermute x4, starting transfers between devices, with_halo(): before = lax.ppermute(last, axis, up)  13.8 us
    ppermute x2, starting transfers between devices, shifted(): lax.ppermute(value, axis, [(source, source + steps) for source in range(l...  9.66 us
  transfers between devices with their start and end apart: 11, of which 9 were waited for; matrix products, arithmetic and copies ran while one was open for 1% of the time, Pallas kernels for 0%

commit v1 on v0

--- a/solution.py
+++ b/solution.py
@@ -87,7 +87,8 @@
         preferred_element_type=jnp.float32,
     ).reshape(latent_count, model_width)
     share_rows = latent_count // lax.axis_size(("cols", "rows"))
-    weighted, row_total = lax.psum((weighted, row_total), ("cols", "rows"))
+    load_turns = lambda raw: lax.psum(lax.psum(raw, "rows"), "cols")
+    weighted, row_total = load_turns((weighted, row_total))
     share_start = lax.axis_index(("cols", "rows")) * share_rows
     weighted = lax.dynamic_slice_in_dim(weighted, share_start, share_rows, 0)
     row_total = lax.dynamic_slice_in_dim(row_total, share_start, share_rows, 0)

time: 332 us -> 356 us (1.072)
  waiting for transfers between devices: 112 us -> 127 us
  blocking collectives: 82.2 us -> 91 us
    psum x1 -> x2, waiting for transfers between devices: 91.8 us -> 107 us  [on_device(): load_turns = lambda raw: lax.psum(lax.psum(raw, 'rows'), 'cols')]
    psum x1 -> x2, blocking collectives: 40.1 us -> 48.8 us  [on_device(): load_turns = lambda raw: lax.psum(lax.psum(raw, 'rows'), 'cols')]
  transfers between devices with their start and end apart: 11 -> 12, of which waited for: 9 -> 10; matrix products, arithmetic and copies ran while one was open for 1% -> 1% of each run, Pallas kernels for 0% -> 0%
where the time goes in v1:
time: 356 us; the launch traced here: 353 us
  waiting for transfers between devices  127 us (36%)
  blocking collectives  91 us (26%)
  local copies, waits for them, and re-layouts  46.5 us (13%)
  matrix products  35.3 us (10%)
  starting transfers between devices  28.8 us (8%)
  between operations  13.8 us (4%)
  other arithmetic  11.4 us (3%)
    psum x2, waiting for transfers between devices, on_device(): load_turns = lambda raw: lax.psum(lax.psum(raw, 'rows'), 'cols')  107 us
    psum x2, blocking collectives, on_device(): load_turns = lambda raw: lax.psum(lax.psum(raw, 'rows'), 'cols')  48.8 us
    pmax x1, blocking collectives, on_device(): peak_score = lax.pmax(jnp.max(scores, axis=2), ('cols', 'rows'))  42.2 us
    conv_general_dilated x11, local copies, waits for them, and re-layouts, convolve(): lax.conv_general_dilated(features[None], kernel, (stride, stride), 'VALID...  32.8 us
    conv_general_dilated x3, matrix products, convolve(): lax.conv_general_dilated(features[None], kernel, (stride, stride), 'VALID...  27.6 us
    ppermute x4, waiting for transfers between devices, with_halo(): after = lax.ppermute(leading, axis, down)  14.5 us
    ppermute x4, starting transfers between devices, with_halo(): before = lax.ppermute(last, axis, up)  13.8 us
    ppermute x2, starting transfers between devices, shifted(): lax.ppermute(value, axis, [(source, source + steps) for source in range(l...  9.66 us
  transfers between devices with their start and end apart: 12, of which 10 were waited for; matrix products, arithmetic and copies ran while one was open for 1% of the time, Pallas kernels for 0%

profile of v1, /device:TPU:0, one launch (start us, length us, event | category | flops | bytes accessed | tf_op | source)
XLA Modules:
  0.0 353.4 jit_solution(13511896727431513970)
XLA Ops:
  7.8 4.9 %collective-permute-start = (bf16[3,256,1]{2,1,0:T(8,128)(2,1)S(1)}, bf16[3,256,1]{2,1,0:T(8,128)(2,1)S(1)}, u32[]{:S(2)}, u32[]{:S(2)}) collective-permute-start(bf16[3,256,1]{2,1,0:T(8,128)(2,1)S(1)} %get-tuple-element.13), channel_id=1, source_target_pairs={{0,4},{4,8},{8,12},{12,16},{16,20},{20,24},{24,28},{1,5},{5,9},{9,... | collective-permute-start | bytes 4616 | tf_op jit(solution)/shard_map/ppermute | solution.py:17
  14.0 2.9 collective-permute-done
  16.9 4.0 %collective-permute-done.1 = bf16[3,256,1]{2,1,0:T(8,128)(2,1)S(1)} collective-permute-done((bf16[3,256,1]{2,1,0:T(8,128)(2,1)S(1)}, bf16[3,256,1]{2,1,0:T(8,128)(2,1)S(1)}, u32[]{:S(2)}, u32[]{:S(2)}) %collective-permute-start.1) | collective-permute-done | bytes 1568 | tf_op jit(solution)/shard_map/ppermute | solution.py:18
  24.4 3.5 collective-permute-done.3
  28.9 2.8 reshape.95
  31.7 19.5 %copy.95 = bf16[3,258,1,8,68]{3,0,4,1,2:T(4,128)(2,1)} copy(bf16[3,258,1,8,68]{4,3,1,0,2:T(8,128)(2,1)} %reshape.95) | data formatting | bytes 1684224 | tf_op jit(solution)/shard_map/conv_general_dilated | solution.py:34
  51.2 2.1 slice.46
  53.3 23.5 %broadcast_select_fusion = f32[64,8,17,64]{3,1,2,0:T(8,128)S(1)} fusion(pred[8,17]{0,1:T(8,128)(4,1)S(1)} %copy-done.5, bf16[6,6,3,64]{3,2,1,0:T(4,128)(2,1)S(1)} %copy-done.4, bf16[3,258,1,7,5]{3,0,4,1,2:T(4,128)(2,1)S(1)} %slice.46, bf16[3,258,1,8,68]{3,0,4,1,2:T(4,128)(2,1)} %copy.95), kind=kOutput, calls=%fused_computation.25 | convolution fusion | flops 123593248 | bytes 3138476 | tf_op jit(solution)/shard_map/conv_general_dilated | solution.py:34
  79.0 4.5 %collective-permute-start.4 = (bf16[64,64,1]{0,1,2:T(8,128)(2,1)S(1)}, bf16[64,64,1]{0,1,2:T(8,128)(2,1)S(1)}, u32[]{:S(2)}, u32[]{:S(2)}) collective-permute-start(bf16[64,64,1]{0,1,2:T(8,128)(2,1)S(1)} %get-tuple-element.7), channel_id=1, source_target_pairs={{0,4},{4,8},{8,12},{12,16},{16,20},{20,24},{24,28},{1,5},{5,9},{9,... | collective-permute-start | bytes 24584 | tf_op jit(solution)/shard_map/ppermute | solution.py:17
  85.0 4.6 %collective-permute-done.5 = bf16[64,64,1]{0,1,2:T(8,128)(2,1)S(1)} collective-permute-done((bf16[64,64,1]{0,1,2:T(8,128)(2,1)S(1)}, bf16[64,64,1]{0,1,2:T(8,128)(2,1)S(1)}, u32[]{:S(2)}, u32[]{:S(2)}) %collective-permute-start.5) | collective-permute-done | bytes 8224 | tf_op jit(solution)/shard_map/ppermute | solution.py:18
  89.7 3.2 collective-permute-start.6
  92.9 1.5 collective-permute-start.7
  94.4 2.3 collective-permute-done.7
  96.7 4.0 %maximum_bitcast_fusion = bf16[64,66,1,130]{0,1,3,2:T(8,128)(2,1)} fusion(bf16[64,1,130]{0,1,2:T(2,128)(2,1)S(1)} %collective-permute-done.7, bf16[64,64,1]{0,1,2:T(8,128)(2,1)S(1)} %collective-permute-done.5, bf16[64,64,128]{0,1,2:T(8,128)(2,1)S(1)} %fusion.14, bf16[64,64,1]{0,1,2:T(8,128)(2,1)S(1)} %collective-permute-done.4, ...), kind=kLoop, calls=%fused_computation.24 | loop fusion | flops 5491200 | bytes 2196480 | tf_op jit(solution)/shard_map/broadcast_in_dim | solution.py:35
  100.7 4.3 %copy.122 = bf16[64,66,1,130]{1,0,3,2:T(8,128)(2,1)} copy(bf16[64,66,1,130]{0,1,3,2:T(8,128)(2,1)} %maximum_bitcast_fusion) | data formatting | bytes 2196480
  105.1 3.9 %pad.2.clone = bf16[64,66,1,160]{1,0,3,2:T(8,128)(2,1)} pad(bf16[64,66,1,130]{1,0,3,2:T(8,128)(2,1)} %copy.122, bf16[]{:T(256)} %constant.41), padding=0_0x0_0x0_0x0_30 | pad | bytes 2449922 | tf_op jit(solution)/shard_map/broadcast_in_dim | solution.py:35
  108.9 4.9 %copy.99 = bf16[64,66,1,8,20]{0,3,4,1,2:T(8,128)(2,1)} copy(bf16[64,66,1,8,20]{1,0,4,3,2:T(8,128)(2,1)} %bitcast.93) | data formatting | bytes 2703360 | tf_op jit(solution)/shard_map/conv_general_dilated | solution.py:34
  113.8 1.4 slice.50
  115.3 3.0 fusion.28
  118.7 4.8 %collective-permute-start.8 = (bf16[1,32,256]{2,0,1:T(2,128)(2,1)S(1)}, bf16[1,32,256]{2,0,1:T(2,128)(2,1)S(1)}, u32[]{:S(2)}, u32[]{:S(2)}) collective-permute-start(bf16[1,32,256]{2,0,1:T(2,128)(2,1)S(1)} %slice.52), channel_id=1, source_target_pairs={{0,1},{1,2},{2,3},{4,5},{5,6},{6,7},{8,9},{9,10},{10,11},{12,13},{... | collective-permute-start | bytes 49160 | tf_op jit(solution)/shard_map/ppermute | solution.py:26
  124.4 4.8 %collective-permute-start.9 = (bf16[17,1,256]{2,0,1:T(8,128)(2,1)S(1)}, bf16[17,1,256]{2,0,1:T(8,128)(2,1)S(1)}, u32[]{:S(2)}, u32[]{:S(2)}) collective-permute-start(bf16[17,1,256]{2,0,1:T(8,128)(2,1)S(1)} %pad_maximum_fusion.3), channel_id=1, source_target_pairs={{0,4},{4,8},{8,12},{12,16},{16,20},{20,24},{24,28},{1,5},{5,9},{9,... | collective-permute-start | bytes 26120 | tf_op jit(solution)/shard_map/ppermute | solution.py:26
  134.7 1.8 bitcast_reduce_fusion
  136.5 42.2 %pmax.7 = f32[8,512]{1,0:T(8,128)S(1)} all-reduce(f32[8,512]{1,0:T(8,128)S(1)} %get-tuple-element.15), channel_id=1, replica_groups=mesh['cols'=8,'rows'=4] {'cols','rows'}, use_global_device_ids=true, to_apply=%region_3.0 | all-reduce | flops 4096 | bytes 32768 | tf_op jit(solution)/shard_map/pmax | solution.py:79
  178.6 2.0 convolution_convert_fusion.1
  180.9 3.4 fusion.33
  184.3 2.9 copy.113
  187.3 51.3 %all-reduce.3.cloned.1.call-done = f32[512,1024]{1,0:T(8,128)} async-done(((f32[512,1024]{1,0:T(8,128)}), f32[512,1024]{1,0:T(8,128)}) %all-reduce.3.cloned.1.call-update) | async-done | bytes 2097168 | tf_op jit(solution)/shard_map/psum | solution.py:90
  238.5 2.0 fusion.25
  240.5 10.1 %psum.30 = f32[512,8]{0,1:T(8,128)S(1)} all-reduce(f32[512,8]{0,1:T(8,128)S(1)} %bitcast.101), channel_id=1, replica_groups=mesh['cols'=8,'rows'=4] {'rows'}, use_global_device_ids=true, to_apply=%region_7.0 | all-reduce | flops 4096 | bytes 32768 | tf_op jit(solution)/shard_map/psum | solution.py:90
  250.6 38.7 %psum.31 = f32[512,8]{0,1:T(8,128)S(1)} all-reduce(f32[512,8]{0,1:T(8,128)S(1)} %psum.30), channel_id=1, replica_groups=mesh['cols'=8,'rows'=4] {'cols'}, use_global_device_ids=true, to_apply=%region_8.0 | all-reduce | flops 4096 | bytes 32768 | tf_op jit(solution)/shard_map/psum | solution.py:90
  289.5 55.5 %all-reduce.5.cloned.1.call-done = f32[512,1024]{1,0:T(8,128)} async-done(((f32[512,1024]{1,0:T(8,128)}), f32[512,1024]{1,0:T(8,128)}) %all-reduce.5.cloned.1.call-update) | async-done | bytes 2097168 | tf_op jit(solution)/shard_map/psum | solution.py:90
  345.1 1.5 fusion.61
  (68 shorter events, 17.8 us)
Async XLA Ops:
  6.5 127.3 %copy-start = (bf16[1024,1024]{1,0:T(8,128)(2,1)S(1)}, bf16[1024,1024]{1,0:T(8,128)(2,1)}, u32[]{:S(2)}) copy-start(bf16[1024,1024]{1,0:T(8,128)(2,1)} %param.11) | copy-start | bytes 6291460
  6.5 21.4 %copy-start.1 = (bf16[3,256,512]{2,1,0:T(8,128)(2,1)S(1)}, bf16[3,256,512]{2,1,0:T(8,128)(2,1)}, u32[]{:S(2)}) copy-start(bf16[3,256,512]{2,1,0:T(8,128)(2,1)} %param.7) | copy-start | bytes 2359300
  6.5 232.0 %all-reduce.3.cloned.1.call-start = ((), (), s32[]{:S(2)}) async-start(), calls=%async_computation | async-start | bytes 4194304 | tf_op jit(solution)/shard_map/psum | solution.py:90
  7.8 9.1 %collective-permute-start = (bf16[3,256,1]{2,1,0:T(8,128)(2,1)S(1)}, bf16[3,256,1]{2,1,0:T(8,128)(2,1)S(1)}, u32[]{:S(2)}, u32[]{:S(2)}) collective-permute-start(bf16[3,256,1]{2,1,0:T(8,128)(2,1)S(1)} %get-tuple-element.13), channel_id=1, source_target_pairs={{0,4},{4,8},{8,12},{12,16},{16,20},{20,24},{24,28},{1,5},{5,9},{9,... | collective-permute-start | bytes 4616 | tf_op jit(solution)/shard_map/ppermute | solution.py:17
  12.7 8.3 %collective-permute-start.1 = (bf16[3,256,1]{2,1,0:T(8,128)(2,1)S(1)}, bf16[3,256,1]{2,1,0:T(8,128)(2,1)S(1)}, u32[]{:S(2)}, u32[]{:S(2)}) collective-permute-start(bf16[3,256,1]{2,1,0:T(8,128)(2,1)S(1)} %get-tuple-element.14), channel_id=1, source_target_pairs={{4,0},{8,4},{12,8},{16,12},{20,16},{24,20},{28,24},{5,1},{9,5},{13... | collective-permute-start | bytes 4616 | tf_op jit(solution)/shard_map/ppermute | solution.py:18
  21.8 2.6 collective-permute-start.2
  23.1 4.8 %collective-permute-start.3 = (bf16[3,1,514]{2,1,0:T(2,128)(2,1)S(1)}, bf16[3,1,514]{2,1,0:T(2,128)(2,1)S(1)}, u32[]{:S(2)}, u32[]{:S(2)}) collective-permute-start(bf16[3,1,514]{2,1,0:T(2,128)(2,1)S(1)} %get-tuple-element.10), channel_id=1, source_target_pairs={{1,0},{2,1},{3,2},{5,4},{6,5},{7,6},{9,8},{10,9},{11,10},{13,12},{... | collective-permute-start | bytes 9260 | tf_op jit(solution)/shard_map/ppermute | solution.py:18
  51.2 2.1 copy-start.4
  51.2 2.1 copy-start.5
  79.0 5.9 %collective-permute-start.4 = (bf16[64,64,1]{0,1,2:T(8,128)(2,1)S(1)}, bf16[64,64,1]{0,1,2:T(8,128)(2,1)S(1)}, u32[]{:S(2)}, u32[]{:S(2)}) collective-permute-start(bf16[64,64,1]{0,1,2:T(8,128)(2,1)S(1)} %get-tuple-element.7), channel_id=1, source_target_pairs={{0,4},{4,8},{8,12},{12,16},{16,20},{20,24},{24,28},{1,5},{5,9},{9,... | collective-permute-start | bytes 24584 | tf_op jit(solution)/shard_map/ppermute | solution.py:17
  83.5 6.1 %collective-permute-start.5 = (bf16[64,64,1]{0,1,2:T(8,128)(2,1)S(1)}, bf16[64,64,1]{0,1,2:T(8,128)(2,1)S(1)}, u32[]{:S(2)}, u32[]{:S(2)}) collective-permute-start(bf16[64,64,1]{0,1,2:T(8,128)(2,1)S(1)} %get-tuple-element.8), channel_id=1, source_target_pairs={{4,0},{8,4},{12,8},{16,12},{20,16},{24,20},{28,24},{5,1},{9,5},{13... | collective-permute-start | bytes 24584 | tf_op jit(solution)/shard_map/ppermute | solution.py:18
  89.7 4.6 %collective-permute-start.6 = (bf16[64,1,130]{0,1,2:T(2,128)(2,1)S(1)}, bf16[64,1,130]{0,1,2:T(2,128)(2,1)S(1)}, u32[]{:S(2)}, u32[]{:S(2)}) collective-permute-start(bf16[64,1,130]{0,1,2:T(2,128)(2,1)S(1)} %get-tuple-element.5), channel_id=1, source_target_pairs={{0,1},{1,2},{2,3},{4,5},{5,6},{6,7},{8,9},{9,10},{10,11},{12,13},{... | collective-permute-start | bytes 49928 | tf_op jit(solution)/shard_map/ppermute | solution.py:17
  92.9 3.8 %collective-permute-start.7 = (bf16[64,1,130]{0,1,2:T(2,128)(2,1)S(1)}, bf16[64,1,130]{0,1,2:T(2,128)(2,1)S(1)}, u32[]{:S(2)}, u32[]{:S(2)}) collective-permute-start(bf16[64,1,130]{0,1,2:T(2,128)(2,1)S(1)} %get-tuple-element.6), channel_id=1, source_target_pairs={{1,0},{2,1},{3,2},{5,4},{6,5},{7,6},{9,8},{10,9},{11,10},{13,12},{... | collective-permute-start | bytes 49928 | tf_op jit(solution)/shard_map/ppermute | solution.py:18
  108.9 6.4 %copy-start.3 = (bf16[6,6,64,256]{3,2,1,0:T(8,128)(2,1)S(1)}, bf16[6,6,64,256]{3,2,1,0:T(8,128)(2,1)}, u32[]{:S(2)}) copy-start(bf16[6,6,64,256]{3,2,1,0:T(8,128)(2,1)} %param.9) | copy-start | bytes 3538948
  108.9 6.4 %copy-start.6 = (pred[8,5]{0,1:T(8,128)(4,1)S(1)}, pred[8,5]{0,1:T(8,128)(4,1)}, u32[]{:S(2)}) copy-start(pred[8,5]{0,1:T(8,128)(4,1)} %constant.54) | copy-start | bytes 124
  113.8 17.2 %slice-start = ((s8[4718592]{0:T(1024)(128)(4,1)}), s8[4194304]{0:T(1024)(128)(4,1)S(1)}, s32[]{:S(2)}) async-start(s8[4718592]{0:T(1024)(128)(4,1)} %bitcast.102), calls=%async_computation.2 | async-start | bytes 8388608
  115.3 15.8 %slice-start.1 = ((s8[4718592]{0:T(1024)(128)(4,1)}), s8[524288]{0:T(1024)(128)(4,1)S(1)}, s32[]{:S(2)}) async-start(s8[4718592]{0:T(1024)(128)(4,1)} %bitcast.102), calls=%async_computation.3 | async-start | bytes 1048576
  118.5 12.6 %copy-start.7 = (pred[8,3]{0,1:T(4,128)(4,1)S(1)}, pred[8,3]{0,1:T(4,128)(4,1)}, u32[]{:S(2)}) copy-start(pred[8,3]{0,1:T(4,128)(4,1)} %constant.53) | copy-start | bytes 76
  118.7 5.7 %collective-permute-start.8 = (bf16[1,32,256]{2,0,1:T(2,128)(2,1)S(1)}, bf16[1,32,256]{2,0,1:T(2,128)(2,1)S(1)}, u32[]{:S(2)}, u32[]{:S(2)}) collective-permute-start(bf16[1,32,256]{2,0,1:T(2,128)(2,1)S(1)} %slice.52), channel_id=1, source_target_pairs={{0,1},{1,2},{2,3},{4,5},{5,6},{6,7},{8,9},{9,10},{10,11},{12,13},{... | collective-permute-start | bytes 49160 | tf_op jit(solution)/shard_map/ppermute | solution.py:26
  124.4 6.2 %collective-permute-start.9 = (bf16[17,1,256]{2,0,1:T(8,128)(2,1)S(1)}, bf16[17,1,256]{2,0,1:T(8,128)(2,1)S(1)}, u32[]{:S(2)}, u32[]{:S(2)}) collective-permute-start(bf16[17,1,256]{2,0,1:T(8,128)(2,1)S(1)} %pad_maximum_fusion.3), channel_id=1, source_target_pairs={{0,4},{4,8},{8,12},{12,16},{16,20},{20,24},{24,28},{1,5},{5,9},{9,... | collective-permute-start | bytes 26120 | tf_op jit(solution)/shard_map/ppermute | solution.py:26
  133.4 1.2 copy-start.2
  187.2 157.8 %all-reduce.5.cloned.1.call-start = ((), (), s32[]{:S(2)}) async-start(), calls=%async_computation.1 | async-start | bytes 4194304 | tf_op jit(solution)/shard_map/psum | solution.py:90
Sparse Core Ops, SparseCore 0:
  187.3 51.1 all-reduce.2
  242.6 102.3 all-reduce.4
